TPU v7x, 32 devices: a whole 2x2x4 slice. The times are simulated.
32 devices in a mesh: grp: 2 (over x), row: 8 (over z, y), col: 2 (over core).
Axes of the slice: x: 2, y: 2, z: 4, core: 2. Of those that a mesh axis runs over, the one named last changes fastest.
Arguments:
- pair_act: bfloat16 [64, 32, 128], P(('grp', 'row'), 'col'), parts along dimension 0, may hold values from -200 to 200
- cotangent: bfloat16 [64, 32, 128], P(('grp', 'row'), 'col'), parts along dimension 0, may hold values from -6 to 6
- residue_mask: int32 [64], P('grp'), parts along dimension 0, may hold values from 0 to 1, as said below
- front_weight: bfloat16 [2, 128, 640], replicated, may hold values from -0.5 to 0.5
- out_weight: bfloat16 [2, 128, 128], replicated, may hold values from -0.5 to 0.5
Outputs:
- pair_grad: bfloat16 [64, 32, 128], P(('grp', 'row'), 'col'), parts along dimension 0
There are 2 independent parts, one for each index of `grp`. A program takes and returns all parts, laid end to end along the dimension named above; an argument that names none is the same for every part. Nothing has to cross between parts.
Inputs may be any that keep to these rules, and one draw needn't show every extreme that they name: residue_mask is 1 on residues 0 to L - 1 and 0 from L on, for a chain length L of at least 24.
All inputs are finite; a program needn't handle non-finite values.
Results may differ from a plain program's by a relative error of at most 0.01.
Values may be sent and summed in bfloat16 or wider, within the bound.
A program may use at most 64 MiB of HBM per device.

v0:
```python
import functools

import jax
import jax.numpy as jnp
from jax import lax
from jax.experimental import pallas as pl
from jax.experimental.pallas import tpu as pltpu
from jax.sharding import PartitionSpec as P

H = 128
TILE = 8
F32 = jnp.float32
BF16 = jnp.bfloat16
MESH = pl.DeviceIdType.MESH
VMEM_BUDGET = 24 << 20
FULL_ARRAYS = 16


def sigmoid(x):
    return 0.5 * jnp.tanh(0.5 * x) + 0.5


def norm(v):
    centred = v - jnp.mean(v, axis=-1, keepdims=True)
    r = lax.rsqrt(jnp.mean(centred * centred, axis=-1, keepdims=True) + 1e-05)
    return centred * r, r


def norm_back(y, r, d):
    return r * (d - jnp.mean(d, axis=-1, keepdims=True) - y * jnp.mean(d * y, axis=-1, keepdims=True))


def rounded(v):
    return v.astype(BF16).astype(F32)


def dot(a, b):
    return jnp.dot(a.astype(BF16), b, preferred_element_type=F32)


def dot_t(a, b):
    return lax.dot_general(
        a.astype(BF16), b, (((1,), (1,)), ((), ())), preferred_element_type=F32
    )


def part(p, n):
    return p[:, n * H : (n + 1) * H]


def flip(value, other, bits):
    total = 0
    for b in range(bits):
        w = 1 << b
        total = total + (value // w + other // w) % 2 * w
    return total


def front_back(x, mask, weight, d_a, d_b, d_gate):
    y, r = norm(x)
    p = dot(y, weight)
    s0, s2, s4 = sigmoid(part(p, 0)), sigmoid(part(p, 2)), sigmoid(part(p, 4))
    ma, mb = d_a * mask * s0, d_b * mask * s2
    d = jnp.concatenate(
        [
            (v.astype(BF16))
            for v in (
                ma * part(p, 1) * (1.0 - s0),
                ma,
                mb * part(p, 3) * (1.0 - s2),
                mb,
                d_gate * s4 * (1.0 - s4),
            )
        ],
        axis=1,
    )
    return rounded(norm_back(y, r, rounded(dot_t(d, weight))))


def crop_kernel(
    rows, pair, cot, mask_in, wf_in, wo_in, out,
    x_all, ct_all, wf, wo, chain, mask, left, right, flipped, mixed, gate, mid,
    in_left, in_right, in_mixed, in_gate, sig, d_left, d_right, ct32, out_sig, grad,
    local_sem, send_sem, recv_sem, fsend_sem, frecv_sem,
):
    n, c = left.shape[0], left.shape[2]
    lr, lc = out.shape[0], out.shape[1]
    bits = rows.bit_length() - 1
    me, my_col = lax.axis_index("row"), lax.axis_index("col")
    other = 1 - my_col
    r0 = pl.multiple_of(me * lr, lr)
    c0 = pl.multiple_of(my_col * lc, lc)

    weights = [
        pltpu.make_async_copy(wf_in, wf, local_sem.at[2]),
        pltpu.make_async_copy(wo_in, wo, local_sem.at[3]),
    ]
    own = []
    for t, (src, dst) in enumerate(((pair, x_all), (cot, ct_all))):
        own.append(
            pltpu.make_async_copy(src, dst.at[pl.ds(r0, lr), pl.ds(c0, lc)], local_sem.at[t])
        )
    chain_copy = pltpu.make_async_copy(mask_in, chain, local_sem.at[4])
    for copy in [chain_copy] + own + weights:
        copy.start()

    barrier = pltpu.get_barrier_semaphore()
    for d in range(1, rows):
        pl.semaphore_signal(
            barrier, inc=1, device_id={"row": flip(me, d, bits)}, device_id_type=MESH
        )
    pl.semaphore_signal(barrier, inc=1, device_id={"col": other}, device_id_type=MESH)

    chain_copy.wait()
    span = jnp.broadcast_to(chain[...].astype(F32), (n, n))
    here = lax.broadcasted_iota(jnp.int32, (n, n), 0) == lax.broadcasted_iota(jnp.int32, (n, n), 1)
    along = jnp.broadcast_to(
        jnp.sum(jnp.where(here, span, 0.0), axis=1, keepdims=True), (n, c)
    )
    flipped[0] = along

    def fill_mask(i, carry):
        mask[i] = along * flipped[0, pl.ds(i, 1), :]
        return carry

    lax.fori_loop(0, n, fill_mask, 0)
    pl.semaphore_wait(barrier, rows)

    def block(ref, row, col):
        return ref.at[
            pl.ds(pl.multiple_of(row * lr, lr), lr), pl.ds(pl.multiple_of(col * lc, lc), lc)
        ]

    def direct(t, d):
        src, dst = ((pair, x_all), (cot, ct_all))[t]
        return pltpu.make_async_remote_copy(
            src_ref=src,
            dst_ref=block(dst, me, my_col),
            send_sem=send_sem.at[t, d],
            recv_sem=recv_sem.at[t, d],
            device_id={"row": flip(me, d, bits)},
            device_id_type=MESH,
        )

    def first(t):
        src, dst = ((pair, x_all), (cot, ct_all))[t]
        return pltpu.make_async_remote_copy(
            src_ref=src,
            dst_ref=block(dst, me, my_col),
            send_sem=fsend_sem.at[t, 0],
            recv_sem=frecv_sem.at[t, 0],
            device_id={"col": other},
            device_id_type=MESH,
        )

    def forward(t, d):
        ref = (x_all, ct_all)[t]
        held = block(ref, flip(me, d, bits), my_col)
        return pltpu.make_async_remote_copy(
            src_ref=held,
            dst_ref=held,
            send_sem=fsend_sem.at[t, d],
            recv_sem=frecv_sem.at[t, d],
            device_id={"col": other},
            device_id_type=MESH,
        )

    def loop(count, step, start=0):
        def body(k, carry):
            step(k)
            return carry

        lax.fori_loop(start, count, body, 0)

    for t in range(2):
        first(t).start()
        loop(rows, lambda d: direct(t, d).start(), 1)

    for copy in weights:
        copy.wait()
    own[0].wait()

    def rows_of(ref, k0, nk):
        return ref[pl.ds(k0, nk)].reshape(nk * n, c)

    def put(ref, k0, nk, v):
        ref[pl.ds(k0, nk)] = v.reshape(nk, n, c)

    def projected(x, k0, nk, weight, a_ref, b_ref, g_ref):
        y, _ = norm(x)
        p = dot(y, weight)
        m = rows_of(mask, k0, nk)
        put(a_ref, k0, nk, rounded(sigmoid(part(p, 0)) * part(p, 1) * m))
        put(b_ref, k0, nk, rounded(sigmoid(part(p, 2)) * part(p, 3) * m))
        put(g_ref, k0, nk, sigmoid(part(p, 4)))

    def arrived(d):
        direct(0, d).wait_recv()
        forward(0, d).start()

    def front_step(g):
        d = 2 * g

        @pl.when(d + 2 < rows)
        def _():
            arrived(d + 2)
            arrived(d + 3)

        forward(0, d).wait_recv()
        forward(0, d + 1).wait_recv()
        k0 = pl.multiple_of(flip(me, d, bits) // 2 * 2 * lr, 2 * lr)
        projected(rows_of(x_all, k0, 2 * lr).astype(F32), k0, 2 * lr, wf[0], left, right, gate)

    arrived(1)
    loop(rows // 2, front_step)

    def transpose(src):
        def step(b):
            i = pl.multiple_of(b * TILE, TILE)
            flipped[:, pl.ds(i, TILE), :] = jnp.swapaxes(src[pl.ds(i, TILE)], 0, 1)

        loop(n // TILE, step)

    def triangle(count, width, row_at, tile_at, store, group):
        def step(b):
            def term(q, acc):
                t = tile_at(q)
                return tuple(v + row_at(b * group + a, q) * t for a, v in enumerate(acc))

            zero = jnp.zeros((width, c), F32)
            acc = lax.fori_loop(0, n, term, (zero,) * group, unroll=True)
            for a in range(group):
                store(b * group + a, acc[a])

        loop(count // group, step)

    transpose(right)

    def put_row(ref):
        def store(a, v):
            ref[a] = v

        return store

    triangle(
        n, n,
        lambda i, k: left[i, pl.ds(k, 1), :],
        lambda k: flipped[k],
        put_row(mixed), 4,
    )

    own[1].wait()

    def pass_on(d):
        direct(1, d).wait_recv()
        forward(1, d).start()

    loop(rows, pass_on, 1)

    some = min(n, 4 * lr)

    def middle_step(b):
        k0 = b * some
        z, _ = norm(rows_of(mixed, k0, some))
        x = rows_of(x_all, k0, some).astype(F32)
        x = rounded(x + rows_of(gate, k0, some) * dot(z, wo[0]))
        put(mid, k0, some, x)
        projected(x, k0, some, wf[1], in_left, in_right, in_gate)

    loop(n // some, middle_step)

    triangle(
        n, n,
        lambda i, k: in_left[k, pl.ds(i, 1), :],
        lambda k: in_right[k],
        put_row(in_mixed), 4,
    )

    loop(rows, lambda d: forward(1, d).wait_recv())

    def signal_step(b):
        k0 = b * some
        z, r = norm(rows_of(in_mixed, k0, some))
        ct = rows_of(ct_all, k0, some).astype(F32)
        put(ct32, k0, some, ct)
        dz = rounded(dot_t(ct * rows_of(in_gate, k0, some), wo[1]))
        put(sig, k0, some, rounded(norm_back(z, r, dz)))

    loop(n // some, signal_step)
    transpose(sig)

    def strip(k0, nk, j0, width, group, chunk):
        def take(ref, k, m):
            return ref[pl.ds(k, m), pl.ds(j0, width), :].reshape(m * width, c)

        def give(ref, k, m, v):
            ref[pl.ds(k, m), pl.ds(j0, width), :] = v.reshape(m, width, c)

        def into(ref):
            def store(a, v):
                ref[k0 + a, pl.ds(j0, width), :] = rounded(v)

            return store

        triangle(
            nk, width,
            lambda a, j: in_right[k0 + a, pl.ds(j, 1), :],
            lambda j: flipped[j, pl.ds(j0, width), :],
            into(d_left), group,
        )
        triangle(
            nk, width,
            lambda a, i: in_left[k0 + a, pl.ds(i, 1), :],
            lambda i: sig[i, pl.ds(j0, width), :],
            into(d_right), group,
        )

        def back(b):
            k = k0 + b * chunk
            ct = take(ct32, k, chunk)
            z1, _ = norm(take(in_mixed, k, chunk))
            d_in = front_back(
                take(mid, k, chunk), take(mask, k, chunk), wf[1],
                take(d_left, k, chunk), take(d_right, k, chunk),
                ct * dot(z1, wo[1]),
            )
            g = rounded(ct + d_in)
            z0, r = norm(take(mixed, k, chunk))
            dz = rounded(dot_t(g * take(gate, k, chunk), wo[0]))
            give(grad, k, chunk, g)
            give(out_sig, k, chunk, rounded(norm_back(z0, r, dz)))

        loop(nk // chunk, back)

    t0 = pl.multiple_of(me * lr // TILE * TILE, TILE)
    strip(r0, lr, 0, n, lr, lr)
    strip(0, n, t0, max(TILE, lr), TILE, 4 * TILE if n % (4 * TILE) == 0 else TILE)

    def own_of(ref):
        def store(a, v):
            ref[r0 + a, pl.ds(c0, lc), :] = rounded(v)

        return store

    triangle(
        lr, lc,
        lambda a, j: out_sig[r0 + a, pl.ds(j, 1), :],
        lambda j: right[j, pl.ds(c0, lc), :],
        own_of(d_left), lr,
    )
    triangle(
        lr, lc,
        lambda a, i: out_sig[i, pl.ds(r0 + a, 1), :],
        lambda i: left[i, pl.ds(c0, lc), :],
        own_of(d_right), lr,
    )

    def mine(ref):
        return ref[pl.ds(r0, lr), pl.ds(c0, lc), :].reshape(lr * lc, c)

    z0, _ = norm(mine(mixed))
    g = mine(grad)
    d_front = front_back(
        mine(x_all).astype(F32), mine(mask), wf[0], mine(d_left), mine(d_right),
        g * dot(z0, wo[0]),
    )
    out[...] = (g + d_front).astype(BF16).reshape(lr, lc, c)

    for t in range(2):
        first(t).wait_send()

        def sent(d):
            direct(t, d).wait_send()
            forward(t, d).wait_send()

        loop(rows, sent, 1)


def from_root(array, axis, root):
    mine = lax.axis_index(axis) == root
    return lax.psum(jnp.where(mine, array, jnp.zeros_like(array)), axis)


def layer_norm(values):
    centred = values - jnp.mean(values, axis=-1, keepdims=True)
    spread = jnp.mean(centred * centred, axis=-1, keepdims=True)
    return centred * lax.rsqrt(spread + 1e-05)


def project_pair(inner_pair, mask_pair, weight):
    normed = layer_norm(inner_pair.astype(jnp.float32)).astype(jnp.bfloat16)
    linear = jnp.dot(normed, weight, preferred_element_type=jnp.float32)
    left_side = jax.nn.sigmoid(linear[..., :H]) * linear[..., H : 2 * H]
    right_side = jax.nn.sigmoid(linear[..., 2 * H : 3 * H]) * linear[..., 3 * H : 4 * H]
    operands = (jnp.stack((left_side, right_side)) * mask_pair[None, :, :, None]).astype(
        jnp.bfloat16
    )
    return (operands, jax.nn.sigmoid(linear[..., 4 * H :]))


def finish(mixed_part, gate_value, inner_pair, weight):
    normed = layer_norm(mixed_part).astype(jnp.bfloat16)
    update = jnp.dot(normed, weight, preferred_element_type=jnp.float32)
    return (inner_pair.astype(jnp.float32) + gate_value * update).astype(jnp.bfloat16)


def body(pair_act, cotangent, residue_mask, front_weight, out_weight):
    local_rows = pair_act.shape[0]
    local_cols = pair_act.shape[1]
    row_index = lax.axis_index("row")
    col_index = lax.axis_index("col")
    block_rows = lax.axis_size("row") // lax.axis_size("col")
    owner_col = row_index // block_rows
    offset = row_index % block_rows * local_rows
    chain_mask = residue_mask.astype(jnp.float32)
    mask_rows = lax.dynamic_slice_in_dim(chain_mask, row_index * local_rows, local_rows)
    mask_cols = lax.dynamic_slice_in_dim(chain_mask, col_index * local_cols, local_cols)
    mask_pair = mask_rows[:, None] * mask_cols[None, :]

    def gather_rows(stacked):
        return lax.all_gather(stacked, "row", axis=1, tiled=True)

    def column_block(gathered):
        slab = lax.dynamic_slice_in_dim(gathered, offset, local_rows, 1)
        return from_root(slab, "col", owner_col)

    def gather_cols(values):
        return lax.all_gather(values, "col", axis=1, tiled=True)

    def sum_cols(partial_term):
        return lax.psum_scatter(
            partial_term.astype(jnp.bfloat16), "col", scatter_dimension=1, tiled=True
        ).astype(jnp.float32)

    (out_ops, out_gate), out_front_back = jax.vjp(
        lambda inner_pair: project_pair(inner_pair, mask_pair, front_weight[0]), pair_act
    )
    fetched = gather_rows(out_ops)
    out_mixed = sum_cols(
        jnp.einsum("ikc,jkc->ijc", out_ops[0], fetched[-1], preferred_element_type=jnp.float32)
    )
    pair_mid, out_finish_back = jax.vjp(
        lambda mixed_part, gate_value, inner_pair: finish(
            mixed_part, gate_value, inner_pair, out_weight[0]
        ),
        out_mixed,
        out_gate,
        pair_act,
    )
    (in_ops, in_gate), in_front_back = jax.vjp(
        lambda inner_pair: project_pair(inner_pair, mask_pair, front_weight[1]), pair_mid
    )
    in_fetched = gather_rows(in_ops)
    left_block = column_block(in_fetched[0])
    in_mixed = jnp.einsum(
        "kic,kjc->ijc", left_block, in_fetched[1], preferred_element_type=jnp.float32
    )
    unused_pair, in_finish_back = jax.vjp(
        lambda mixed_part, gate_value, inner_pair: finish(
            mixed_part, gate_value, inner_pair, out_weight[1]
        ),
        in_mixed,
        in_gate,
        pair_mid,
    )
    grad_mixed, grad_gate, grad_inner = in_finish_back(cotangent)
    signal = grad_mixed.astype(jnp.bfloat16)
    signal_rows = gather_rows(signal[None])[0]
    left_rows = gather_cols(in_ops[0])
    grad_right = jnp.einsum(
        "kic,ijc->kjc", left_rows, signal_rows, preferred_element_type=jnp.float32
    )
    grad_left = sum_cols(
        jnp.einsum("kjc,ijc->kic", in_ops[1], signal_rows, preferred_element_type=jnp.float32)
    )
    (grad_front,) = in_front_back(
        (jnp.stack((grad_left, grad_right)).astype(jnp.bfloat16), grad_gate)
    )
    grad_mid = (grad_inner.astype(jnp.float32) + grad_front.astype(jnp.float32)).astype(
        jnp.bfloat16
    )
    grad_mixed, grad_gate, grad_inner = out_finish_back(grad_mid)
    signal = grad_mixed.astype(jnp.bfloat16)
    signal_cols = gather_cols(signal)
    grad_left = jnp.einsum(
        "ijc,jkc->ikc", signal_cols, fetched[-1], preferred_element_type=jnp.float32
    )
    signal_block = column_block(gather_rows(signal[None])[0])
    grad_right = jnp.einsum(
        "ijc,ikc->jkc", signal_block, fetched[0], preferred_element_type=jnp.float32
    )
    (grad_front,) = out_front_back(
        (jnp.stack((grad_left, grad_right)).astype(jnp.bfloat16), grad_gate)
    )
    return (grad_inner.astype(jnp.float32) + grad_front.astype(jnp.float32)).astype(jnp.bfloat16)


def crop_body(rows, pair_act, cotangent, residue_mask, front_weight, out_weight):
    lr, lc, c = pair_act.shape
    n = residue_mask.shape[0]
    full = pltpu.VMEM((n, n, c), F32)
    dma = pltpu.SemaphoreType.DMA
    hbm = pl.BlockSpec(memory_space=pl.ANY)
    return pl.pallas_call(
        functools.partial(crop_kernel, rows),
        out_shape=jax.ShapeDtypeStruct((lr, lc, c), BF16),
        in_specs=[hbm] * 5,
        out_specs=pl.BlockSpec(memory_space=pltpu.VMEM),
        scratch_shapes=[
            pltpu.VMEM((n, n, c), BF16),
            pltpu.VMEM((n, n, c), BF16),
            pltpu.VMEM(front_weight.shape, BF16),
            pltpu.VMEM(out_weight.shape, BF16),
            pltpu.VMEM((1, n), jnp.int32),
        ]
        + [full] * 17
        + [dma((5,)), dma((2, rows)), dma((2, rows)), dma((2, rows)), dma((2, rows))],
        compiler_params=pltpu.CompilerParams(
            collective_id=0, has_side_effects=True, vmem_limit_bytes=67043328
        ),
    )(pair_act, cotangent, residue_mask.reshape(1, n), front_weight, out_weight)


def fits(mesh, n, lr, lc, c):
    rows, cols = mesh.shape["row"], mesh.shape["col"]
    return (
        cols == 2
        and rows >= 2
        and rows & (rows - 1) == 0
        and n % TILE == 0
        and (lr % TILE == 0 or TILE % lr == 0)
        and lc % (2 * TILE) == 0
        and FULL_ARRAYS * 4 * n * n * c <= VMEM_BUDGET
    )


def solution(mesh):
    def dispatch(pair_act, cotangent, residue_mask, front_weight, out_weight):
        n = residue_mask.shape[0]
        if fits(mesh, n, *pair_act.shape):
            return crop_body(
                mesh.shape["row"], pair_act, cotangent, residue_mask, front_weight, out_weight
            )
        return body(pair_act, cotangent, residue_mask, front_weight, out_weight)

    placed = (P(("grp", "row"), "col", None), P(("grp", "row"), "col", None), P("grp"), P(), P())
    return jax.shard_map(
        dispatch,
        mesh=mesh,
        in_specs=placed,
        out_specs=P(("grp", "row"), "col", None),
        check_vma=False,
    )
```

profile of v0, /device:TPU:0, one launch (start us, length us, event | category | flops | bytes accessed | tf_op | source)
XLA Modules:
  0.0 24.4 jit_solution(11843626278375729660)
XLA Ops:
  0.0 23.1 %shard_map.55 = bf16[4,16,128]{2,1,0:T(8,128)(2,1)} custom-call(bf16[4,16,128]{2,1,0:T(8,128)(2,1)} %pair.1, bf16[4,16,128]{2,1,0:T(8,128)(2,1)} %cot.1, s32[1,32]{1,0:T(1,128)} %bitcast.1, bf16[2,128,640]{2,1,0:T(8,128)(2,1)} %wf_in.1, bf16[2,128,128]{2,1,0:T(8,128)(2,1)} %wo_in.1), custom_call_target="tpu_custom_call" | custom-call | tf_op jit(solution)/shard_map/pallas_call | solution.py:504
  23.1 1.3 %copy.7 = bf16[4,16,128]{2,1,0:T(8,128)(2,1)} copy(bf16[4,16,128]{2,1,0:T(8,128)(2,1)} %shard_map.55) | data formatting | bytes 32768
where the time goes:
time: 24.9 us; the launch traced here: 24.4 us
  Pallas kernels  23.1 us (93%)
  local copies, waits for them, and re-layouts  1.32 us (5%)
    pallas_call x1, Pallas kernels, crop_body(): pl.pallas_call(functools.partial(crop_kernel, rows), out_shape=jax.ShapeD...  23.1 us
    unnamed x1, local copies, waits for them, and re-layouts  1.32 us

commit v1 on v0

--- a/solution.py
+++ b/solution.py
@@ -516,9 +516,9 @@
         + [full] * 17
         + [dma((5,)), dma((2, rows)), dma((2, rows)), dma((2, rows)), dma((2, rows))],
         compiler_params=pltpu.CompilerParams(
-            collective_id=0, has_side_effects=True, vmem_limit_bytes=67043328
+            collective_id=0, has_side_effects=True, vmem_limit_bytes=24 << 20
         ),
-    )(pair_act, cotangent, residue_mask.reshape(1, n), front_weight, out_weight)
+    )(*[pltpu.with_memory_space_constraint(v, pltpu.HBM) for v in (pair_act, cotangent, residue_mask.reshape(1, n), front_weight, out_weight)])
 
 
 def fits(mesh, n, lr, lc, c):

time: 24.9 us -> 23.5 us (0.944)
  local copies, waits for them, and re-layouts: 1.32 us -> 0.61 us
  Pallas kernels: 23.1 us -> 22.5 us
    unnamed x1, local copies, waits for them, and re-layouts: 1.32 us -> 0.61 us
    pallas_call x1, Pallas kernels: 23.1 us -> 22.5 us  [crop_body(): pl.pallas_call(functools.partial(crop_kernel, rows), out_shape=jax.ShapeD...]
where the time goes in v1:
time: 23.5 us; the launch traced here: 23.1 us
  Pallas kernels  22.5 us (96%)
  local copies, waits for them, and re-layouts  0.61 us (3%)
    pallas_call x1, Pallas kernels, crop_body(): pl.pallas_call(functools.partial(crop_kernel, rows), out_shape=jax.ShapeD...  22.5 us
    unnamed x1, local copies, waits for them, and re-layouts  0.61 us

profile of v1, /device:TPU:0, one launch (start us, length us, event | category | flops | bytes accessed | tf_op | source)
XLA Modules:
  0.0 23.1 jit_solution(18200856452153258410)
XLA Ops:
  0.0 22.5 %shard_map.55 = bf16[4,16,128]{2,1,0:T(8,128)(2,1)S(1)} custom-call(bf16[4,16,128]{2,1,0:T(8,128)(2,1)} %pair.1, bf16[4,16,128]{2,1,0:T(8,128)(2,1)} %cot.1, s32[1,32]{1,0:T(1,128)} %bitcast.1, bf16[2,128,640]{2,1,0:T(8,128)(2,1)} %wf_in.1, bf16[2,128,128]{2,1,0:T(8,128)(2,1)} %wo_in.1), custom_call_target="tpu_custom_call" | custom-call | tf_op jit(solution)/shard_map/pallas_call | solution.py:504
  22.5 0.6 %copy.7 = bf16[4,16,128]{2,1,0:T(8,128)(2,1)} copy(bf16[4,16,128]{2,1,0:T(8,128)(2,1)S(1)} %shard_map.55) | data formatting | bytes 32768

commit v2 on v1

v2 whole, which is shorter than its diff:
```python
import functools

import jax
import jax.numpy as jnp
from jax import lax
from jax.experimental import pallas as pl
from jax.experimental.pallas import tpu as pltpu
from jax.sharding import PartitionSpec as P

H = 128
TILE = 8
F32 = jnp.float32
BF16 = jnp.bfloat16
MESH = pl.DeviceIdType.MESH
VMEM_BUDGET = 24 << 20
FULL_ARRAYS = 16


def sigmoid(x):
    return 0.5 * jnp.tanh(0.5 * x) + 0.5


def norm(v):
    centred = v - jnp.mean(v, axis=-1, keepdims=True)
    r = lax.rsqrt(jnp.mean(centred * centred, axis=-1, keepdims=True) + 1e-05)
    return centred * r, r


def norm_back(y, r, d):
    return r * (d - jnp.mean(d, axis=-1, keepdims=True) - y * jnp.mean(d * y, axis=-1, keepdims=True))


def rounded(v):
    return v.astype(BF16).astype(F32)


def dot(a, b):
    return jnp.dot(a.astype(BF16), b, preferred_element_type=F32)


def dot_t(a, b):
    return lax.dot_general(
        a.astype(BF16), b, (((1,), (1,)), ((), ())), preferred_element_type=F32
    )


def part(p, n):
    return p[:, n * H : (n + 1) * H]


def factors(x, mask, weight):
    y, r = norm(x)
    p = dot(y, weight)
    s0, s2, s4 = sigmoid(part(p, 0)), sigmoid(part(p, 2)), sigmoid(part(p, 4))
    fa, fb = mask * s0, mask * s2
    return y, r, fa * part(p, 1) * (1.0 - s0), fa, fb * part(p, 3) * (1.0 - s2), fb, s4 * (1.0 - s4)


def front_back(f, weight, d_a, d_b, d_gate):
    y, r, f0, f1, f2, f3, f4 = f
    d = jnp.concatenate(
        [(v.astype(BF16)) for v in (d_a * f0, d_a * f1, d_b * f2, d_b * f3, d_gate * f4)], axis=1
    )
    return rounded(norm_back(y, r, rounded(dot_t(d, weight))))


def crop_kernel(
    rows, pair, cot, mask_in, wf_in, wo_in, out,
    x_h, ct_h, wf, wo, chain,
    left, right, in_left, in_right, sig, left_t, right_t, flip_r, flip_s,
    mask, mixed, gate, mid, in_mixed, in_gate, ct32, along,
    saved, d_left, d_right, sig_row, sig_col,
    local_sem, send_sem, recv_sem, psend, precv,
):
    n, c = left.shape[0], left.shape[2]
    lr, lc = out.shape[0], out.shape[1]
    bits = rows.bit_length() - 1
    me, my_col = lax.axis_index("row"), lax.axis_index("col")
    other = 1 - my_col
    me_bits = [lax.rem(lax.div(me, 1 << b), 2) for b in range(bits)]

    def flip(d, low=0):
        total = 0
        for b in range(low, bits):
            bit = me_bits[b]
            total = total + (1 - bit if d >> b & 1 else bit) * (1 << b)
        return total

    barrier = pltpu.get_barrier_semaphore()
    for d in range(1, rows):
        pl.semaphore_signal(barrier, inc=1, device_id={"row": flip(d)}, device_id_type=MESH)
    pl.semaphore_signal(barrier, inc=1, device_id={"col": other}, device_id_type=MESH)

    r0 = pl.multiple_of(me * lr, lr)
    c0 = pl.multiple_of(my_col * lc, lc)
    o0 = pl.multiple_of(other * lc, lc)
    jl = lax.rem(me * lr, lc)
    owner = lax.div(me * lr, lc) == my_col

    own = [
        pltpu.make_async_copy(src, dst.at[pl.ds(r0, lr)], local_sem.at[t])
        for t, (src, dst) in enumerate(((pair, x_h), (cot, ct_h)))
    ]
    weights = [
        pltpu.make_async_copy(wf_in, wf, local_sem.at[2]),
        pltpu.make_async_copy(wo_in, wo, local_sem.at[3]),
    ]
    chain_copy = pltpu.make_async_copy(mask_in, chain, local_sem.at[4])
    for copy in [chain_copy, own[0]] + weights + [own[1]]:
        copy.start()

    def direct(t, d):
        src, dst = ((pair, x_h), (cot, ct_h))[t]
        return pltpu.make_async_remote_copy(
            src_ref=src,
            dst_ref=dst.at[pl.ds(r0, lr)],
            send_sem=send_sem.at[t, d],
            recv_sem=recv_sem.at[t, d],
            device_id={"row": flip(d)},
            device_id_type=MESH,
        )

    used = []

    def partner(src, dst=None):
        q = len(used)
        copy = pltpu.make_async_remote_copy(
            src_ref=src,
            dst_ref=src if dst is None else dst,
            send_sem=psend.at[q],
            recv_sem=precv.at[q],
            device_id={"col": other},
            device_id_type=MESH,
        )
        used.append(copy)
        return copy

    pl.semaphore_wait(barrier, rows)
    for t in range(2):
        for d in range(1, rows):
            direct(t, d).start()

    chain_copy.wait()
    span = jnp.broadcast_to(chain[...].astype(F32), (n, n))
    here = lax.broadcasted_iota(jnp.int32, (n, n), 0) == lax.broadcasted_iota(jnp.int32, (n, n), 1)
    along[...] = jnp.broadcast_to(
        jnp.sum(jnp.where(here, span, 0.0), axis=1, keepdims=True), (n, c)
    )
    across = along[pl.ds(c0, lc), :]
    for i in range(n):
        mask[i * lc : (i + 1) * lc] = across * along[i : i + 1]

    def block(ref, k0, nk):
        return ref[pl.ds(pl.multiple_of(k0 * lc, lc), nk * lc), :]

    def put(ref, k0, nk, v):
        ref[pl.ds(pl.multiple_of(k0 * lc, lc), nk * lc), :] = v

    def put_half(ref, k0, nk, v):
        ref[pl.ds(k0, nk), pl.ds(c0, lc), :] = v.reshape(nk, lc, c)

    def half(ref, k0, nk):
        return ref.at[pl.ds(k0, nk), pl.ds(c0, lc)]

    def projected(x, k0, nk, weight, a_ref, b_ref, g_ref):
        y, _ = norm(x)
        p = dot(y, weight)
        m = block(mask, k0, nk)
        put_half(a_ref, k0, nk, rounded(sigmoid(part(p, 0)) * part(p, 1) * m))
        put_half(b_ref, k0, nk, rounded(sigmoid(part(p, 2)) * part(p, 3) * m))
        put(g_ref, k0, nk, sigmoid(part(p, 4)))

    def triangle(count, width, first, depth, row_at, tile_at, acc=None):
        def term(q, acc):
            t = tile_at(first + q)
            return tuple(v + row_at(a, first + q) * t for a, v in enumerate(acc))

        if acc is None:
            acc = (jnp.zeros((width, c), F32),) * count
        return lax.fori_loop(0, depth, term, tuple(acc), unroll=True)

    def loop(count, step):
        def body(k, carry):
            step(k)
            return carry

        lax.fori_loop(0, count, body, 0)

    for copy in weights:
        copy.wait()
    two = 2 * lr
    e_left, e_right = [], []
    for g in range(rows // 2):
        k0 = pl.multiple_of(flip(2 * g, 1) * lr, two)
        if g == 0:
            own[0].wait()
            direct(0, 1).wait_recv()
        else:
            direct(0, 2 * g).wait_recv()
            direct(0, 2 * g + 1).wait_recv()
        x = x_h[pl.ds(k0, two)].reshape(two * lc, c).astype(F32)
        projected(x, k0, two, wf[0], left, right, gate)
        e_left.append(partner(half(left, k0, two)))
        e_right.append(partner(half(right, k0, two)))
        e_left[-1].start()
        e_right[-1].start()

    group = TILE

    def outgoing(k0, fresh):
        for b in range(lc // TILE):
            t = jnp.swapaxes(right[pl.ds(c0 + b * TILE, TILE), pl.ds(k0, lc), :], 0, 1)
            flip_r[:, b * TILE : (b + 1) * TILE, :] = t

        def step(b):
            i0 = b * group
            base = pl.multiple_of(i0 * lc, lc * group)
            acc = None
            if not fresh:
                acc = [mixed[pl.ds(base + a * lc, lc), :] for a in range(group)]
            acc = triangle(
                group, lc, 0, lc,
                lambda a, q: left[i0 + a, pl.ds(k0 + q, 1), :],
                lambda q: flip_r[q],
                acc,
            )
            for a in range(group):
                mixed[pl.ds(base + a * lc, lc), :] = acc[a]

        loop(n // group, step)

    outgoing(c0, True)
    for copy in e_left + e_right:
        copy.wait_recv()
    outgoing(o0, False)

    some = n // 2
    e_in = []
    for b in range(2):
        k0 = b * some
        z, _ = norm(block(mixed, k0, some))
        x = x_h[pl.ds(k0, some)].reshape(some * lc, c).astype(F32)
        x = rounded(x + block(gate, k0, some) * dot(z, wo[0]))
        put(mid, k0, some, x)
        projected(x, k0, some, wf[1], in_left, in_right, in_gate)
        e_in.append(partner(half(in_left, k0, some)))
        e_in[-1].start()
    e_right = [partner(half(in_right, 0, n))]
    e_right[0].start()

    def incoming(i0):
        def step(b):
            i1 = pl.multiple_of(i0 + b * group, group)
            acc = triangle(
                group, lc, 0, n,
                lambda a, q: in_left[q, pl.ds(i1 + a, 1), :],
                lambda q: in_right[q, pl.ds(c0, lc), :],
            )
            for a in range(group):
                in_mixed[pl.ds(pl.multiple_of((i1 + a) * lc, lc), lc), :] = acc[a]

        loop(lc // group, step)

    nr, nc = lr * lc, lr * n

    def row_of(ref):
        return ref[pl.ds(pl.multiple_of(r0 * lc, lc), nr), :]

    def col_of(ref):
        return jnp.concatenate([ref[pl.ds(jl + a, n, stride=lc), :] for a in range(lr)], axis=0)

    def strips(ref, wide):
        return jnp.concatenate([row_of(ref), col_of(ref)], axis=0) if wide else row_of(ref)

    def each(step):
        @pl.when(owner)
        def _():
            step(True, nr + nc)

        @pl.when(jnp.logical_not(owner))
        def _():
            step(False, nr)

    def transposed(src, dst, j0):
        for b in range(n // TILE):
            t = jnp.swapaxes(src[b * TILE : (b + 1) * TILE, pl.ds(j0, lc), :], 0, 1)
            dst[pl.ds(j0, lc), b * TILE : (b + 1) * TILE, :] = t

    incoming(c0)

    def prepare(wide, m):
        f = factors(strips(mid, wide), strips(mask, wide), wf[1])
        for q, v in enumerate(f):
            saved[q, :m] = jnp.broadcast_to(v, (m, c))
        if wide:
            transposed(in_left, left_t, c0)
            transposed(in_right, right_t, c0)

    each(prepare)
    for copy in e_in:
        copy.wait_recv()
    incoming(o0)

    for d in range(1, rows):
        direct(1, d).wait_recv()
    own[1].wait()

    def signal(i0):
        z, r = norm(block(in_mixed, i0, lc))
        ct = ct_h[pl.ds(i0, lc)].reshape(lc * lc, c).astype(F32)
        put(ct32, i0, lc, ct)
        dz = rounded(dot_t(ct * block(in_gate, i0, lc), wo[1]))
        put_half(sig, i0, lc, rounded(norm_back(z, r, dz)))

    signal(o0)
    e_sig = partner(half(sig, o0, lc))
    e_sig.start()
    signal(c0)
    e_right[0].wait_recv()

    def turn_signal(j0):
        for b in range(lc // TILE):
            t = jnp.swapaxes(sig[pl.ds(c0 + b * TILE, TILE), pl.ds(j0, lc), :], 0, 1)
            flip_s[:, b * TILE : (b + 1) * TILE, :] = t

    def left_row(j0, acc):
        return triangle(
            lr, lc, 0, lc,
            lambda a, q: in_right[r0 + a, pl.ds(j0 + q, 1), :],
            lambda q: flip_s[q],
            acc,
        )

    def left_col(j0, acc):
        return triangle(
            lr, n, 0, lc,
            lambda a, q: sig[r0 + a, pl.ds(j0 + q, 1), :],
            lambda q: right_t[j0 + q],
            acc,
        )

    def keep(ref, start, width, acc, fix=lambda v: v):
        for a in range(lr):
            ref[start + a * width : start + (a + 1) * width] = fix(acc[a])

    def kept(ref, start, width):
        return [ref[start + a * width : start + (a + 1) * width] for a in range(lr)]

    turn_signal(c0)
    keep(d_right, 0, lc, triangle(
        lr, lc, 0, n,
        lambda a, q: in_left[r0 + a, pl.ds(q, 1), :],
        lambda q: sig[q, pl.ds(c0, lc), :],
    ), rounded)
    keep(d_left, 0, lc, left_row(c0, None))

    @pl.when(owner)
    def _():
        transposed(in_left, left_t, o0)
        transposed(in_right, right_t, o0)
        keep(d_right, nr, n, triangle(
            lr, n, 0, n,
            lambda a, q: sig[q, pl.ds(r0 + a, 1), :],
            lambda q: left_t[q],
        ), rounded)
        keep(d_left, nr, n, left_col(c0, None))

    def prepare_more(wide, m):
        z1, _ = norm(strips(in_mixed, wide))
        saved[7, :m] = strips(ct32, wide) * dot(z1, wo[1])

    each(prepare_more)
    e_sig.wait_recv()
    turn_signal(o0)
    keep(d_left, 0, lc, left_row(o0, kept(d_left, 0, lc)), rounded)

    @pl.when(owner)
    def _():
        keep(d_left, nr, n, left_col(o0, kept(d_left, nr, n)), rounded)

    def back(wide, m):
        f = tuple(saved[q, :m] for q in range(7))
        g = rounded(strips(ct32, wide) + front_back(f, wf[1], d_left[:m], d_right[:m], saved[7, :m]))
        z0, r = norm(strips(mixed, wide))
        dz = rounded(dot_t(g * strips(gate, wide), wo[0]))
        s = rounded(norm_back(z0, r, dz))
        along_row = s[:nr].reshape(lr, lc, c)
        sig_row[:, pl.ds(c0, lc), :] = along_row
        saved[8, :nr] = g[:nr]
        if wide:
            sig_col[...] = s[nr:].reshape(lr, n, c)

    each(back)
    e_row = partner(sig_row.at[:, pl.ds(c0, lc)])
    e_row.start()
    e_col = partner(sig_col)

    @pl.when(owner)
    def _():
        e_col.start()

    x = x_h[pl.ds(r0, lr)].reshape(nr, c).astype(F32)
    f = factors(x, row_of(mask), wf[0])
    z0, _ = norm(row_of(mixed))
    g = saved[8, :nr]
    d_gate = g * dot(z0, wo[0])

    def out_left(j0, acc):
        return triangle(
            lr, lc, 0, lc,
            lambda a, q: sig_row[a, pl.ds(j0 + q, 1), :],
            lambda q: right[j0 + q, pl.ds(c0, lc), :],
            acc,
        )

    acc = out_left(c0, None)
    e_row.wait_recv()
    d_a = jnp.concatenate([rounded(v) for v in out_left(o0, acc)], axis=0)

    @pl.when(jnp.logical_not(owner))
    def _():
        e_col.wait_recv()

    d_b = jnp.concatenate([rounded(v) for v in triangle(
        lr, lc, 0, n,
        lambda a, q: sig_col[a, pl.ds(q, 1), :],
        lambda q: left[q, pl.ds(c0, lc), :],
    )], axis=0)
    out[...] = (g + front_back(f, wf[0], d_a, d_b, d_gate)).astype(BF16).reshape(lr, lc, c)

    for t in range(2):
        for d in range(1, rows):
            direct(t, d).wait_send()
    for copy in used:
        if copy is not e_col:
            copy.wait_send()

    @pl.when(owner)
    def _():
        e_col.wait_send()


def from_root(array, axis, root):
    mine = lax.axis_index(axis) == root
    return lax.psum(jnp.where(mine, array, jnp.zeros_like(array)), axis)


def layer_norm(values):
    centred = values - jnp.mean(values, axis=-1, keepdims=True)
    spread = jnp.mean(centred * centred, axis=-1, keepdims=True)
    return centred * lax.rsqrt(spread + 1e-05)


def project_pair(inner_pair, mask_pair, weight):
    normed = layer_norm(inner_pair.astype(jnp.float32)).astype(jnp.bfloat16)
    linear = jnp.dot(normed, weight, preferred_element_type=jnp.float32)
    left_side = jax.nn.sigmoid(linear[..., :H]) * linear[..., H : 2 * H]
    right_side = jax.nn.sigmoid(linear[..., 2 * H : 3 * H]) * linear[..., 3 * H : 4 * H]
    operands = (jnp.stack((left_side, right_side)) * mask_pair[None, :, :, None]).astype(
        jnp.bfloat16
    )
    return (operands, jax.nn.sigmoid(linear[..., 4 * H :]))


def finish(mixed_part, gate_value, inner_pair, weight):
    normed = layer_norm(mixed_part).astype(jnp.bfloat16)
    update = jnp.dot(normed, weight, preferred_element_type=jnp.float32)
    return (inner_pair.astype(jnp.float32) + gate_value * update).astype(jnp.bfloat16)


def body(pair_act, cotangent, residue_mask, front_weight, out_weight):
    local_rows = pair_act.shape[0]
    local_cols = pair_act.shape[1]
    row_index = lax.axis_index("row")
    col_index = lax.axis_index("col")
    block_rows = lax.axis_size("row") // lax.axis_size("col")
    owner_col = row_index // block_rows
    offset = row_index % block_rows * local_rows
    chain_mask = residue_mask.astype(jnp.float32)
    mask_rows = lax.dynamic_slice_in_dim(chain_mask, row_index * local_rows, local_rows)
    mask_cols = lax.dynamic_slice_in_dim(chain_mask, col_index * local_cols, local_cols)
    mask_pair = mask_rows[:, None] * mask_cols[None, :]

    def gather_rows(stacked):
        return lax.all_gather(stacked, "row", axis=1, tiled=True)

    def column_block(gathered):
        slab = lax.dynamic_slice_in_dim(gathered, offset, local_rows, 1)
        return from_root(slab, "col", owner_col)

    def gather_cols(values):
        return lax.all_gather(values, "col", axis=1, tiled=True)

    def sum_cols(partial_term):
        return lax.psum_scatter(
            partial_term.astype(jnp.bfloat16), "col", scatter_dimension=1, tiled=True
        ).astype(jnp.float32)

    (out_ops, out_gate), out_front_back = jax.vjp(
        lambda inner_pair: project_pair(inner_pair, mask_pair, front_weight[0]), pair_act
    )
    fetched = gather_rows(out_ops)
    out_mixed = sum_cols(
        jnp.einsum("ikc,jkc->ijc", out_ops[0], fetched[-1], preferred_element_type=jnp.float32)
    )
    pair_mid, out_finish_back = jax.vjp(
        lambda mixed_part, gate_value, inner_pair: finish(
            mixed_part, gate_value, inner_pair, out_weight[0]
        ),
        out_mixed,
        out_gate,
        pair_act,
    )
    (in_ops, in_gate), in_front_back = jax.vjp(
        lambda inner_pair: project_pair(inner_pair, mask_pair, front_weight[1]), pair_mid
    )
    in_fetched = gather_rows(in_ops)
    left_block = column_block(in_fetched[0])
    in_mixed = jnp.einsum(
        "kic,kjc->ijc", left_block, in_fetched[1], preferred_element_type=jnp.float32
    )
    unused_pair, in_finish_back = jax.vjp(
        lambda mixed_part, gate_value, inner_pair: finish(
            mixed_part, gate_value, inner_pair, out_weight[1]
        ),
        in_mixed,
        in_gate,
        pair_mid,
    )
    grad_mixed, grad_gate, grad_inner = in_finish_back(cotangent)
    signal = grad_mixed.astype(jnp.bfloat16)
    signal_rows = gather_rows(signal[None])[0]
    left_rows = gather_cols(in_ops[0])
    grad_right = jnp.einsum(
        "kic,ijc->kjc", left_rows, signal_rows, preferred_element_type=jnp.float32
    )
    grad_left = sum_cols(
        jnp.einsum("kjc,ijc->kic", in_ops[1], signal_rows, preferred_element_type=jnp.float32)
    )
    (grad_front,) = in_front_back(
        (jnp.stack((grad_left, grad_right)).astype(jnp.bfloat16), grad_gate)
    )
    grad_mid = (grad_inner.astype(jnp.float32) + grad_front.astype(jnp.float32)).astype(
        jnp.bfloat16
    )
    grad_mixed, grad_gate, grad_inner = out_finish_back(grad_mid)
    signal = grad_mixed.astype(jnp.bfloat16)
    signal_cols = gather_cols(signal)
    grad_left = jnp.einsum(
        "ijc,jkc->ikc", signal_cols, fetched[-1], preferred_element_type=jnp.float32
    )
    signal_block = column_block(gather_rows(signal[None])[0])
    grad_right = jnp.einsum(
        "ijc,ikc->jkc", signal_block, fetched[0], preferred_element_type=jnp.float32
    )
    (grad_front,) = out_front_back(
        (jnp.stack((grad_left, grad_right)).astype(jnp.bfloat16), grad_gate)
    )
    return (grad_inner.astype(jnp.float32) + grad_front.astype(jnp.float32)).astype(jnp.bfloat16)


def crop_body(rows, pair_act, cotangent, residue_mask, front_weight, out_weight):
    lr, lc, c = pair_act.shape
    n = residue_mask.shape[0]
    strip = lr * lc + lr * n
    dma = pltpu.SemaphoreType.DMA
    copies = rows + 6
    operands = (pair_act, cotangent, residue_mask.reshape(1, n), front_weight, out_weight)
    return pl.pallas_call(
        functools.partial(crop_kernel, rows),
        out_shape=jax.ShapeDtypeStruct((lr, lc, c), BF16),
        in_specs=[pl.BlockSpec(memory_space=pl.ANY)] * 5,
        out_specs=pl.BlockSpec(memory_space=pltpu.VMEM),
        scratch_shapes=[
            pltpu.VMEM((n, lc, c), BF16),
            pltpu.VMEM((n, lc, c), BF16),
            pltpu.VMEM(front_weight.shape, BF16),
            pltpu.VMEM(out_weight.shape, BF16),
            pltpu.VMEM((1, n), jnp.int32),
        ]
        + [pltpu.VMEM((n, n, c), F32)] * 7
        + [pltpu.VMEM((lc, lc, c), F32)] * 2
        + [pltpu.VMEM((n * lc, c), F32)] * 7
        + [
            pltpu.VMEM((n, c), F32),
            pltpu.VMEM((9, strip, c), F32),
            pltpu.VMEM((strip, c), F32),
            pltpu.VMEM((strip, c), F32),
            pltpu.VMEM((lr, n, c), F32),
            pltpu.VMEM((lr, n, c), F32),
        ]
        + [dma((5,)), dma((2, rows)), dma((2, rows)), dma((copies,)), dma((copies,))],
        compiler_params=pltpu.CompilerParams(
            collective_id=0, has_side_effects=True, vmem_limit_bytes=VMEM_BUDGET
        ),
    )(*[pltpu.with_memory_space_constraint(v, pltpu.HBM) for v in operands])


def fits(mesh, n, lr, lc, c):
    rows, cols = mesh.shape["row"], mesh.shape["col"]
    return (
        cols == 2
        and rows >= 2
        and rows & (rows - 1) == 0
        and n == 2 * lc
        and lc % (2 * TILE) == 0
        and lc % (2 * lr) == 0
        and FULL_ARRAYS * 4 * n * n * c <= VMEM_BUDGET
    )


def solution(mesh):
    def dispatch(pair_act, cotangent, residue_mask, front_weight, out_weight):
        n = residue_mask.shape[0]
        if fits(mesh, n, *pair_act.shape):
            return crop_body(
                mesh.shape["row"], pair_act, cotangent, residue_mask, front_weight, out_weight
            )
        return body(pair_act, cotangent, residue_mask, front_weight, out_weight)

    placed = (P(("grp", "row"), "col", None), P(("grp", "row"), "col", None), P("grp"), P(), P())
    return jax.shard_map(
        dispatch,
        mesh=mesh,
        in_specs=placed,
        out_specs=P(("grp", "row"), "col", None),
        check_vma=False,
    )
```

time: 23.5 us -> 20.5 us (0.87)
  Pallas kernels: 22.5 us -> 19.7 us
    pallas_call x1, Pallas kernels: 22.5 us -> 19.7 us  [crop_body(): pl.pallas_call(functools.partial(crop_kernel, rows), out_shape=jax.ShapeD...]
where the time goes in v2:
time: 20.5 us; the launch traced here: 20.3 us
  Pallas kernels  19.7 us (96%)
  local copies, waits for them, and re-layouts  0.61 us (3%)
    pallas_call x1, Pallas kernels, crop_body(): pl.pallas_call(functools.partial(crop_kernel, rows), out_shape=jax.ShapeD...  19.7 us
    unnamed x1, local copies, waits for them, and re-layouts  0.61 us

profile of v2, /device:TPU:0, one launch (start us, length us, event | category | flops | bytes accessed | tf_op | source)
XLA Modules:
  0.0 20.3 jit_solution(1729103366715315416)
XLA Ops:
  0.0 19.7 %shard_map.55 = bf16[4,16,128]{2,1,0:T(8,128)(2,1)S(1)} custom-call(bf16[4,16,128]{2,1,0:T(8,128)(2,1)} %pair.1, bf16[4,16,128]{2,1,0:T(8,128)(2,1)} %cot.1, s32[1,32]{1,0:T(1,128)} %bitcast.1, bf16[2,128,640]{2,1,0:T(8,128)(2,1)} %wf_in.1, bf16[2,128,128]{2,1,0:T(8,128)(2,1)} %wo_in.1), custom_call_target="tpu_custom_call" | custom-call | tf_op jit(solution)/shard_map/pallas_call | solution.py:569
  19.7 0.6 %copy.7 = bf16[4,16,128]{2,1,0:T(8,128)(2,1)} copy(bf16[4,16,128]{2,1,0:T(8,128)(2,1)S(1)} %shard_map.55) | data formatting | bytes 32768

commit v3 on v2

--- a/solution.py
+++ b/solution.py
@@ -70,7 +70,7 @@
     left, right, in_left, in_right, sig, left_t, right_t, flip_r, flip_s,
     mask, mixed, gate, mid, in_mixed, in_gate, ct32, along,
     saved, d_left, d_right, sig_row, sig_col,
-    local_sem, send_sem, recv_sem, psend, precv,
+    local_sem, send_sem, recv_sem, psend, precv, ready,
 ):
     n, c = left.shape[0], left.shape[2]
     lr, lc = out.shape[0], out.shape[1]
@@ -87,9 +87,11 @@
         return total
 
     barrier = pltpu.get_barrier_semaphore()
-    for d in range(1, rows):
-        pl.semaphore_signal(barrier, inc=1, device_id={"row": flip(d)}, device_id_type=MESH)
     pl.semaphore_signal(barrier, inc=1, device_id={"col": other}, device_id_type=MESH)
+    for row in range(1, rows):
+        @pl.when(me < row)
+        def _():
+            pl.semaphore_signal(barrier, inc=1, device_id={"row": row}, device_id_type=MESH)
 
     r0 = pl.multiple_of(me * lr, lr)
     c0 = pl.multiple_of(my_col * lc, lc)
@@ -109,16 +111,43 @@
     for copy in [chain_copy, own[0]] + weights + [own[1]]:
         copy.start()
 
-    def direct(t, d):
+    def direct(t, row, mine=None):
         src, dst = ((pair, x_h), (cot, ct_h))[t]
+        source = row if mine is None else mine
         return pltpu.make_async_remote_copy(
             src_ref=src,
-            dst_ref=dst.at[pl.ds(r0, lr)],
-            send_sem=send_sem.at[t, d],
-            recv_sem=recv_sem.at[t, d],
-            device_id={"row": flip(d)},
+            dst_ref=dst.at[pl.ds(pl.multiple_of(source * lr, lr), lr)],
+            send_sem=send_sem.at[t, row],
+            recv_sem=recv_sem.at[t, source],
+            device_id={"row": row},
             device_id_type=MESH,
         )
+
+    def lower(step):
+        for row in range(rows - 1):
+            @pl.when(row < me)
+            def _():
+                step(row)
+
+    def higher(step):
+        for row in range(1, rows):
+            @pl.when(row > me)
+            def _():
+                step(row)
+
+    def answer(row):
+        pl.semaphore_signal(ready.at[me], inc=1, device_id={"row": row}, device_id_type=MESH)
+        direct(0, row, me).start()
+
+    def follow(row):
+        pl.semaphore_wait(ready.at[row], 1)
+        direct(0, row, me).start()
+
+    def drain(row):
+        direct(0, row, me).wait_send()
+
+    def second(row):
+        direct(1, row, me).start()
 
     used = []
 
@@ -135,10 +164,8 @@
         used.append(copy)
         return copy
 
-    pl.semaphore_wait(barrier, rows)
-    for t in range(2):
-        for d in range(1, rows):
-            direct(t, d).start()
+    pl.semaphore_wait(barrier, me + 1)
+    lower(answer)
 
     chain_copy.wait()
     span = jnp.broadcast_to(chain[...].astype(F32), (n, n))
@@ -162,13 +189,20 @@
     def half(ref, k0, nk):
         return ref.at[pl.ds(k0, nk), pl.ds(c0, lc)]
 
-    def projected(x, k0, nk, weight, a_ref, b_ref, g_ref):
+    def projected(x, segments, weight, a_ref, b_ref, g_ref):
         y, _ = norm(x)
         p = dot(y, weight)
-        m = block(mask, k0, nk)
-        put_half(a_ref, k0, nk, rounded(sigmoid(part(p, 0)) * part(p, 1) * m))
-        put_half(b_ref, k0, nk, rounded(sigmoid(part(p, 2)) * part(p, 3) * m))
-        put(g_ref, k0, nk, sigmoid(part(p, 4)))
+        m = jnp.concatenate([block(mask, k0, nk) for k0, nk in segments], axis=0)
+        a = rounded(sigmoid(part(p, 0)) * part(p, 1) * m)
+        b = rounded(sigmoid(part(p, 2)) * part(p, 3) * m)
+        g = sigmoid(part(p, 4))
+        at = 0
+        for k0, nk in segments:
+            span = slice(at * lc, (at + nk) * lc)
+            put_half(a_ref, k0, nk, a[span])
+            put_half(b_ref, k0, nk, b[span])
+            put(g_ref, k0, nk, g[span])
+            at += nk
 
     def triangle(count, width, first, depth, row_at, tile_at, acc=None):
         def term(q, acc):
@@ -188,22 +222,35 @@
 
     for copy in weights:
         copy.wait()
-    two = 2 * lr
     e_left, e_right = [], []
-    for g in range(rows // 2):
-        k0 = pl.multiple_of(flip(2 * g, 1) * lr, two)
+    groups = [[(0, 1)], [(1, 1), (2, 2)], [(4, 2)], [(6, 2)]]
+    for g, group in enumerate(groups):
+        for d, count in group:
+            for q in range(d, d + count):
+                if q == 0:
+                    own[0].wait()
+                else:
+                    direct(0, flip(q)).wait_recv()
+        segments = [
+            (pl.multiple_of(flip(d, count.bit_length() - 1) * lr, count * lr), count * lr)
+            for d, count in group
+        ]
+        x = jnp.concatenate(
+            [x_h[pl.ds(k0, nk)].reshape(nk * lc, c).astype(F32) for k0, nk in segments], axis=0
+        )
+        projected(x, segments, wf[0], left, right, gate)
+        for k0, nk in segments:
+            e_left.append(partner(half(left, k0, nk)))
+            e_right.append(partner(half(right, k0, nk)))
+            e_left[-1].start()
+            e_right[-1].start()
         if g == 0:
-            own[0].wait()
-            direct(0, 1).wait_recv()
-        else:
-            direct(0, 2 * g).wait_recv()
-            direct(0, 2 * g + 1).wait_recv()
-        x = x_h[pl.ds(k0, two)].reshape(two * lc, c).astype(F32)
-        projected(x, k0, two, wf[0], left, right, gate)
-        e_left.append(partner(half(left, k0, two)))
-        e_right.append(partner(half(right, k0, two)))
-        e_left[-1].start()
-        e_right[-1].start()
+            higher(follow)
+            lower(drain)
+            e_left[0].wait_recv()
+            lower(second)
+        if g == 3:
+            higher(second)
 
     group = TILE
 
@@ -230,7 +277,7 @@
         loop(n // group, step)
 
     outgoing(c0, True)
-    for copy in e_left + e_right:
+    for copy in e_left[1:] + e_right:
         copy.wait_recv()
     outgoing(o0, False)
 
@@ -242,7 +289,7 @@
         x = x_h[pl.ds(k0, some)].reshape(some * lc, c).astype(F32)
         x = rounded(x + block(gate, k0, some) * dot(z, wo[0]))
         put(mid, k0, some, x)
-        projected(x, k0, some, wf[1], in_left, in_right, in_gate)
+        projected(x, [(k0, some)], wf[1], in_left, in_right, in_gate)
         e_in.append(partner(half(in_left, k0, some)))
         e_in[-1].start()
     e_right = [partner(half(in_right, 0, n))]
@@ -302,7 +349,7 @@
     incoming(o0)
 
     for d in range(1, rows):
-        direct(1, d).wait_recv()
+        direct(1, flip(d)).wait_recv()
     own[1].wait()
 
     def signal(i0):
@@ -428,9 +475,9 @@
     )], axis=0)
     out[...] = (g + front_back(f, wf[0], d_a, d_b, d_gate)).astype(BF16).reshape(lr, lc, c)
 
-    for t in range(2):
-        for d in range(1, rows):
-            direct(t, d).wait_send()
+    higher(drain)
+    for d in range(1, rows):
+        direct(1, flip(d)).wait_send()
     for copy in used:
         if copy is not e_col:
             copy.wait_send()
@@ -564,7 +611,7 @@
     n = residue_mask.shape[0]
     strip = lr * lc + lr * n
     dma = pltpu.SemaphoreType.DMA
-    copies = rows + 6
+    copies = 2 * rows + 6
     operands = (pair_act, cotangent, residue_mask.reshape(1, n), front_weight, out_weight)
     return pl.pallas_call(
         functools.partial(crop_kernel, rows),
@@ -589,7 +636,8 @@
             pltpu.VMEM((lr, n, c), F32),
             pltpu.VMEM((lr, n, c), F32),
         ]
-        + [dma((5,)), dma((2, rows)), dma((2, rows)), dma((copies,)), dma((copies,))],
+        + [dma((5,)), dma((2, rows)), dma((2, rows)), dma((copies,)), dma((copies,))]
+        + [pltpu.SemaphoreType.REGULAR((rows,))],
         compiler_params=pltpu.CompilerParams(
             collective_id=0, has_side_effects=True, vmem_limit_bytes=VMEM_BUDGET
         ),

time: 20.5 us -> 18.4 us (0.90)
  Pallas kernels: 19.7 us -> 17.7 us
    pallas_call x1, Pallas kernels: 19.7 us -> 17.7 us  [crop_body(): pl.pallas_call(functools.partial(crop_kernel, rows), out_shape=jax.ShapeD...]
where the time goes in v3:
time: 18.4 us; the launch traced here: 18.3 us
  Pallas kernels  17.7 us (96%)
  local copies, waits for them, and re-layouts  0.61 us (3%)
    pallas_call x1, Pallas kernels, crop_body(): pl.pallas_call(functools.partial(crop_kernel, rows), out_shape=jax.ShapeD...  17.7 us
    unnamed x1, local copies, waits for them, and re-layouts  0.61 us

profile of v3, /device:TPU:0, one launch (start us, length us, event | category | flops | bytes accessed | tf_op | source)
XLA Modules:
  0.0 18.3 jit_solution(2262759261694598300)
XLA Ops:
  0.0 17.7 %shard_map.55 = bf16[4,16,128]{2,1,0:T(8,128)(2,1)S(1)} custom-call(bf16[4,16,128]{2,1,0:T(8,128)(2,1)} %pair.1, bf16[4,16,128]{2,1,0:T(8,128)(2,1)} %cot.1, s32[1,32]{1,0:T(1,128)} %bitcast.1, bf16[2,128,640]{2,1,0:T(8,128)(2,1)} %wf_in.1, bf16[2,128,128]{2,1,0:T(8,128)(2,1)} %wo_in.1), custom_call_target="tpu_custom_call" | custom-call | tf_op jit(solution)/shard_map/pallas_call | solution.py:616
  17.7 0.6 %copy.7 = bf16[4,16,128]{2,1,0:T(8,128)(2,1)} copy(bf16[4,16,128]{2,1,0:T(8,128)(2,1)S(1)} %shard_map.55) | data formatting | bytes 32768

commit v4 on v3

--- a/solution.py
+++ b/solution.py
@@ -68,9 +68,9 @@
     rows, pair, cot, mask_in, wf_in, wo_in, out,
     x_h, ct_h, wf, wo, chain,
     left, right, in_left, in_right, sig, left_t, right_t, flip_r, flip_s,
-    mask, mixed, gate, mid, in_mixed, in_gate, ct32, along,
+    mask, mixed, gate, mid, in_mixed, in_gate, ct32, normed, along,
     saved, d_left, d_right, sig_row, sig_col,
-    local_sem, send_sem, recv_sem, psend, precv, ready,
+    local_sem, x_send, x_recv, ct_send, ct_recv, psend, precv, ready,
 ):
     n, c = left.shape[0], left.shape[2]
     lr, lc = out.shape[0], out.shape[1]
@@ -117,8 +117,8 @@
         return pltpu.make_async_remote_copy(
             src_ref=src,
             dst_ref=dst.at[pl.ds(pl.multiple_of(source * lr, lr), lr)],
-            send_sem=send_sem.at[t, row],
-            recv_sem=recv_sem.at[t, source],
+            send_sem=x_send.at[row] if t == 0 else ct_send.at[0],
+            recv_sem=x_recv.at[source] if t == 0 else ct_recv.at[0],
             device_id={"row": row},
             device_id_type=MESH,
         )
@@ -136,8 +136,13 @@
                 step(row)
 
     def answer(row):
+        if row < 2:
+            direct(0, row, me).start()
         pl.semaphore_signal(ready.at[me], inc=1, device_id={"row": row}, device_id_type=MESH)
-        direct(0, row, me).start()
+
+    def send(row):
+        if row >= 2:
+            direct(0, row, me).start()
 
     def follow(row):
         pl.semaphore_wait(ready.at[row], 1)
@@ -149,20 +154,15 @@
     def second(row):
         direct(1, row, me).start()
 
-    used = []
-
-    def partner(src, dst=None):
-        q = len(used)
-        copy = pltpu.make_async_remote_copy(
-            src_ref=src,
-            dst_ref=src if dst is None else dst,
+    def partner(q, ref):
+        return pltpu.make_async_remote_copy(
+            src_ref=ref,
+            dst_ref=ref,
             send_sem=psend.at[q],
             recv_sem=precv.at[q],
             device_id={"col": other},
             device_id_type=MESH,
         )
-        used.append(copy)
-        return copy
 
     pl.semaphore_wait(barrier, me + 1)
     lower(answer)
@@ -176,6 +176,7 @@
     across = along[pl.ds(c0, lc), :]
     for i in range(n):
         mask[i * lc : (i + 1) * lc] = across * along[i : i + 1]
+    lower(send)
 
     def block(ref, k0, nk):
         return ref[pl.ds(pl.multiple_of(k0 * lc, lc), nk * lc), :]
@@ -222,8 +223,8 @@
 
     for copy in weights:
         copy.wait()
-    e_left, e_right = [], []
-    groups = [[(0, 1)], [(1, 1), (2, 2)], [(4, 2)], [(6, 2)]]
+    groups = [[(0, 1)], [(1, 1), (2, 2)] if rows > 2 else [(1, 1)]]
+    groups += [[(d, 2)] for d in range(4, rows, 2)]
     for g, group in enumerate(groups):
         for d, count in group:
             for q in range(d, d + count):
@@ -240,16 +241,14 @@
         )
         projected(x, segments, wf[0], left, right, gate)
         for k0, nk in segments:
-            e_left.append(partner(half(left, k0, nk)))
-            e_right.append(partner(half(right, k0, nk)))
-            e_left[-1].start()
-            e_right[-1].start()
+            partner(0 if g == 0 else 1, half(left, k0, nk)).start()
+            partner(2, half(right, k0, nk)).start()
         if g == 0:
             higher(follow)
             lower(drain)
-            e_left[0].wait_recv()
+            partner(0, half(left, r0, lr)).wait_recv()
             lower(second)
-        if g == 3:
+        if g == len(groups) - 1:
             higher(second)
 
     group = TILE
@@ -277,23 +276,27 @@
         loop(n // group, step)
 
     outgoing(c0, True)
-    for copy in e_left[1:] + e_right:
-        copy.wait_recv()
+    e_left = [partner(0, half(left, r0, lr)), partner(1, half(left, 0, n - lr))]
+    e_right = partner(2, half(right, 0, n))
+    e_left[1].wait_recv()
+    e_right.wait_recv()
     outgoing(o0, False)
 
-    some = n // 2
-    e_in = []
-    for b in range(2):
-        k0 = b * some
-        z, _ = norm(block(mixed, k0, some))
-        x = x_h[pl.ds(k0, some)].reshape(some * lc, c).astype(F32)
-        x = rounded(x + block(gate, k0, some) * dot(z, wo[0]))
-        put(mid, k0, some, x)
-        projected(x, [(k0, some)], wf[1], in_left, in_right, in_gate)
-        e_in.append(partner(half(in_left, k0, some)))
-        e_in[-1].start()
-    e_right = [partner(half(in_right, 0, n))]
-    e_right[0].start()
+    z, _ = norm(mixed[...])
+    x = x_h[...].reshape(n * lc, c).astype(F32)
+    x = rounded(x + gate[...] * dot(z, wo[0]))
+    mid[...] = x
+    y = norm(x)[0].astype(BF16)
+    normed[...] = y
+    p = dot(y, wf[1, :, : 2 * H])
+    put_half(in_left, 0, n, rounded(sigmoid(part(p, 0)) * part(p, 1) * mask[...]))
+    e_in_left = partner(3, half(in_left, 0, n))
+    e_in_left.start()
+    p = dot(normed[...], wf[1, :, 2 * H :])
+    put_half(in_right, 0, n, rounded(sigmoid(part(p, 0)) * part(p, 1) * mask[...]))
+    in_gate[...] = sigmoid(part(p, 2))
+    e_in_right = partner(4, half(in_right, 0, n))
+    e_in_right.start()
 
     def incoming(i0):
         def step(b):
@@ -319,12 +322,12 @@
     def strips(ref, wide):
         return jnp.concatenate([row_of(ref), col_of(ref)], axis=0) if wide else row_of(ref)
 
-    def each(step):
-        @pl.when(owner)
+    def each(step, here=True):
+        @pl.when(jnp.logical_and(here, owner))
         def _():
             step(True, nr + nc)
 
-        @pl.when(jnp.logical_not(owner))
+        @pl.when(jnp.logical_and(here, jnp.logical_not(owner)))
         def _():
             step(False, nr)
 
@@ -339,17 +342,27 @@
         f = factors(strips(mid, wide), strips(mask, wide), wf[1])
         for q, v in enumerate(f):
             saved[q, :m] = jnp.broadcast_to(v, (m, c))
-        if wide:
-            transposed(in_left, left_t, c0)
-            transposed(in_right, right_t, c0)
-
-    each(prepare)
-    for copy in e_in:
-        copy.wait_recv()
+
+    each(prepare, my_col == 0)
+
+    @pl.when(jnp.logical_and(my_col == 0, owner))
+    def _():
+        transposed(in_left, left_t, c0)
+        transposed(in_right, right_t, c0)
+
+    e_in_left.wait_recv()
     incoming(o0)
 
-    for d in range(1, rows):
-        direct(1, flip(d)).wait_recv()
+    others = pl.ds(0, (rows - 1) * lr)
+    e_ct = pltpu.make_async_remote_copy(
+        src_ref=ct_h.at[others],
+        dst_ref=ct_h.at[others],
+        send_sem=ct_send.at[0],
+        recv_sem=ct_recv.at[0],
+        device_id={"col": other},
+        device_id_type=MESH,
+    )
+    e_ct.wait_recv()
     own[1].wait()
 
     def signal(i0):
@@ -360,10 +373,10 @@
         put_half(sig, i0, lc, rounded(norm_back(z, r, dz)))
 
     signal(o0)
-    e_sig = partner(half(sig, o0, lc))
+    e_sig = partner(5, half(sig, o0, lc))
     e_sig.start()
     signal(c0)
-    e_right[0].wait_recv()
+    e_in_right.wait_recv()
 
     def turn_signal(j0):
         for b in range(lc // TILE):
@@ -403,6 +416,11 @@
 
     @pl.when(owner)
     def _():
+        @pl.when(my_col != 0)
+        def _():
+            transposed(in_left, left_t, c0)
+            transposed(in_right, right_t, c0)
+
         transposed(in_left, left_t, o0)
         transposed(in_right, right_t, o0)
         keep(d_right, nr, n, triangle(
@@ -416,6 +434,7 @@
         z1, _ = norm(strips(in_mixed, wide))
         saved[7, :m] = strips(ct32, wide) * dot(z1, wo[1])
 
+    each(prepare, my_col == 1)
     each(prepare_more)
     e_sig.wait_recv()
     turn_signal(o0)
@@ -438,9 +457,9 @@
             sig_col[...] = s[nr:].reshape(lr, n, c)
 
     each(back)
-    e_row = partner(sig_row.at[:, pl.ds(c0, lc)])
+    e_row = partner(6, sig_row.at[:, pl.ds(c0, lc)])
     e_row.start()
-    e_col = partner(sig_col)
+    e_col = partner(7, sig_col)
 
     @pl.when(owner)
     def _():
@@ -476,11 +495,9 @@
     out[...] = (g + front_back(f, wf[0], d_a, d_b, d_gate)).astype(BF16).reshape(lr, lc, c)
 
     higher(drain)
-    for d in range(1, rows):
-        direct(1, flip(d)).wait_send()
-    for copy in used:
-        if copy is not e_col:
-            copy.wait_send()
+    e_ct.wait_send()
+    for copy in e_left + [e_right, e_in_left, e_in_right, e_sig, e_row]:
+        copy.wait_send()
 
     @pl.when(owner)
     def _():
@@ -611,7 +628,6 @@
     n = residue_mask.shape[0]
     strip = lr * lc + lr * n
     dma = pltpu.SemaphoreType.DMA
-    copies = 2 * rows + 6
     operands = (pair_act, cotangent, residue_mask.reshape(1, n), front_weight, out_weight)
     return pl.pallas_call(
         functools.partial(crop_kernel, rows),
@@ -629,6 +645,7 @@
         + [pltpu.VMEM((lc, lc, c), F32)] * 2
         + [pltpu.VMEM((n * lc, c), F32)] * 7
         + [
+            pltpu.VMEM((n * lc, c), BF16),
             pltpu.VMEM((n, c), F32),
             pltpu.VMEM((9, strip, c), F32),
             pltpu.VMEM((strip, c), F32),
@@ -636,7 +653,7 @@
             pltpu.VMEM((lr, n, c), F32),
             pltpu.VMEM((lr, n, c), F32),
         ]
-        + [dma((5,)), dma((2, rows)), dma((2, rows)), dma((copies,)), dma((copies,))]
+        + [dma((5,)), dma((rows,)), dma((rows,)), dma((1,)), dma((1,)), dma((8,)), dma((8,))]
         + [pltpu.SemaphoreType.REGULAR((rows,))],
         compiler_params=pltpu.CompilerParams(
             collective_id=0, has_side_effects=True, vmem_limit_bytes=VMEM_BUDGET

time: 18.4 us -> 17.6 us (0.957)
  Pallas kernels: 17.7 us -> 16.9 us
    pallas_call x1, Pallas kernels: 17.7 us -> 16.9 us  [crop_body(): pl.pallas_call(functools.partial(crop_kernel, rows), out_shape=jax.ShapeD...]
where the time goes in v4:
time: 17.6 us; the launch traced here: 17.5 us
  Pallas kernels  16.9 us (96%)
  local copies, waits for them, and re-layouts  0.61 us (3%)
    pallas_call x1, Pallas kernels, crop_body(): pl.pallas_call(functools.partial(crop_kernel, rows), out_shape=jax.ShapeD...  16.9 us
    unnamed x1, local copies, waits for them, and re-layouts  0.61 us

profile of v4, /device:TPU:0, one launch (start us, length us, event | category | flops | bytes accessed | tf_op | source)
XLA Modules:
  0.0 17.5 jit_solution(7546779176503514498)
XLA Ops:
  0.0 16.9 %shard_map.55 = bf16[4,16,128]{2,1,0:T(8,128)(2,1)S(1)} custom-call(bf16[4,16,128]{2,1,0:T(8,128)(2,1)} %pair.1, bf16[4,16,128]{2,1,0:T(8,128)(2,1)} %cot.1, s32[1,32]{1,0:T(1,128)} %bitcast.1, bf16[2,128,640]{2,1,0:T(8,128)(2,1)} %wf_in.1, bf16[2,128,128]{2,1,0:T(8,128)(2,1)} %wo_in.1), custom_call_target="tpu_custom_call" | custom-call | tf_op jit(solution)/shard_map/pallas_call | solution.py:632
  16.9 0.6 %copy.7 = bf16[4,16,128]{2,1,0:T(8,128)(2,1)} copy(bf16[4,16,128]{2,1,0:T(8,128)(2,1)S(1)} %shard_map.55) | data formatting | bytes 32768

commit v5 on v4

--- a/solution.py
+++ b/solution.py
@@ -154,12 +154,12 @@
     def second(row):
         direct(1, row, me).start()
 
-    def partner(q, ref):
+    def partner(q, r, ref):
         return pltpu.make_async_remote_copy(
             src_ref=ref,
             dst_ref=ref,
             send_sem=psend.at[q],
-            recv_sem=precv.at[q],
+            recv_sem=precv.at[r],
             device_id={"col": other},
             device_id_type=MESH,
         )
@@ -241,12 +241,15 @@
         )
         projected(x, segments, wf[0], left, right, gate)
         for k0, nk in segments:
-            partner(0 if g == 0 else 1, half(left, k0, nk)).start()
-            partner(2, half(right, k0, nk)).start()
+            partner(0, 0, half(left, k0, nk)).start()
+            partner(0, 0, half(right, k0, nk)).start()
         if g == 0:
             higher(follow)
             lower(drain)
-            partner(0, half(left, r0, lr)).wait_recv()
+            pl.semaphore_signal(
+                ready.at[rows], inc=1, device_id={"col": other}, device_id_type=MESH
+            )
+            pl.semaphore_wait(ready.at[rows], 1)
             lower(second)
         if g == len(groups) - 1:
             higher(second)
@@ -276,10 +279,8 @@
         loop(n // group, step)
 
     outgoing(c0, True)
-    e_left = [partner(0, half(left, r0, lr)), partner(1, half(left, 0, n - lr))]
-    e_right = partner(2, half(right, 0, n))
-    e_left[1].wait_recv()
-    e_right.wait_recv()
+    e_out = partner(0, 0, left)
+    e_out.wait_recv()
     outgoing(o0, False)
 
     z, _ = norm(mixed[...])
@@ -290,26 +291,34 @@
     normed[...] = y
     p = dot(y, wf[1, :, : 2 * H])
     put_half(in_left, 0, n, rounded(sigmoid(part(p, 0)) * part(p, 1) * mask[...]))
-    e_in_left = partner(3, half(in_left, 0, n))
-    e_in_left.start()
+    e_in_left = [
+        partner(1, 1 + b, in_left.at[:, pl.ds(c0 + b * TILE, TILE)]) for b in range(lc // TILE)
+    ]
+    for copy in e_in_left:
+        copy.start()
     p = dot(normed[...], wf[1, :, 2 * H :])
     put_half(in_right, 0, n, rounded(sigmoid(part(p, 0)) * part(p, 1) * mask[...]))
     in_gate[...] = sigmoid(part(p, 2))
-    e_in_right = partner(4, half(in_right, 0, n))
+    e_in_right = partner(1, 3, half(in_right, 0, n))
     e_in_right.start()
 
-    def incoming(i0):
-        def step(b):
-            i1 = pl.multiple_of(i0 + b * group, group)
+    def incoming(i0, copies=()):
+        few = 4
+
+        def step(i1):
             acc = triangle(
-                group, lc, 0, n,
+                few, lc, 0, n,
                 lambda a, q: in_left[q, pl.ds(i1 + a, 1), :],
                 lambda q: in_right[q, pl.ds(c0, lc), :],
             )
-            for a in range(group):
+            for a in range(few):
                 in_mixed[pl.ds(pl.multiple_of((i1 + a) * lc, lc), lc), :] = acc[a]
 
-        loop(lc // group, step)
+        for b in range(lc // TILE):
+            if copies:
+                copies[b].wait_recv()
+            for a in range(0, TILE, few):
+                step(pl.multiple_of(i0 + b * TILE, TILE) + a)
 
     nr, nc = lr * lc, lr * n
 
@@ -350,8 +359,7 @@
         transposed(in_left, left_t, c0)
         transposed(in_right, right_t, c0)
 
-    e_in_left.wait_recv()
-    incoming(o0)
+    incoming(o0, e_in_left)
 
     others = pl.ds(0, (rows - 1) * lr)
     e_ct = pltpu.make_async_remote_copy(
@@ -373,7 +381,7 @@
         put_half(sig, i0, lc, rounded(norm_back(z, r, dz)))
 
     signal(o0)
-    e_sig = partner(5, half(sig, o0, lc))
+    e_sig = partner(2, 4, half(sig, o0, lc))
     e_sig.start()
     signal(c0)
     e_in_right.wait_recv()
@@ -457,9 +465,9 @@
             sig_col[...] = s[nr:].reshape(lr, n, c)
 
     each(back)
-    e_row = partner(6, sig_row.at[:, pl.ds(c0, lc)])
+    e_row = partner(3, 5, sig_row.at[:, pl.ds(c0, lc)])
     e_row.start()
-    e_col = partner(7, sig_col)
+    e_col = partner(4, 6, sig_col)
 
     @pl.when(owner)
     def _():
@@ -496,7 +504,7 @@
 
     higher(drain)
     e_ct.wait_send()
-    for copy in e_left + [e_right, e_in_left, e_in_right, e_sig, e_row]:
+    for copy in (e_out, partner(1, 3, in_left), e_sig, e_row):
         copy.wait_send()
 
     @pl.when(owner)
@@ -653,8 +661,8 @@
             pltpu.VMEM((lr, n, c), F32),
             pltpu.VMEM((lr, n, c), F32),
         ]
-        + [dma((5,)), dma((rows,)), dma((rows,)), dma((1,)), dma((1,)), dma((8,)), dma((8,))]
-        + [pltpu.SemaphoreType.REGULAR((rows,))],
+        + [dma((5,)), dma((rows,)), dma((rows,)), dma((1,)), dma((1,)), dma((5,)), dma((7,))]
+        + [pltpu.SemaphoreType.REGULAR((rows + 1,))],
         compiler_params=pltpu.CompilerParams(
             collective_id=0, has_side_effects=True, vmem_limit_bytes=VMEM_BUDGET
         ),
@@ -668,7 +676,7 @@
         and rows >= 2
         and rows & (rows - 1) == 0
         and n == 2 * lc
-        and lc % (2 * TILE) == 0
+        and lc == 2 * TILE
         and lc % (2 * lr) == 0
         and FULL_ARRAYS * 4 * n * n * c <= VMEM_BUDGET
     )

time: 17.6 us -> 17.3 us (0.983)
  Pallas kernels: 16.9 us -> 16.5 us
    pallas_call x1, Pallas kernels: 16.9 us -> 16.5 us  [crop_body(): pl.pallas_call(functools.partial(crop_kernel, rows), out_shape=jax.ShapeD...]
where the time goes in v5:
time: 17.3 us; the launch traced here: 17.2 us
  Pallas kernels  16.5 us (95%)
  local copies, waits for them, and re-layouts  0.61 us (4%)
    pallas_call x1, Pallas kernels, crop_body(): pl.pallas_call(functools.partial(crop_kernel, rows), out_shape=jax.ShapeD...  16.5 us
    unnamed x1, local copies, waits for them, and re-layouts  0.61 us

profile of v5, /device:TPU:0, one launch (start us, length us, event | category | flops | bytes accessed | tf_op | source)
XLA Modules:
  0.0 17.2 jit_solution(17675942883864857028)
XLA Ops:
  0.0 16.5 %shard_map.55 = bf16[4,16,128]{2,1,0:T(8,128)(2,1)S(1)} custom-call(bf16[4,16,128]{2,1,0:T(8,128)(2,1)} %pair.1, bf16[4,16,128]{2,1,0:T(8,128)(2,1)} %cot.1, s32[1,32]{1,0:T(1,128)} %bitcast.1, bf16[2,128,640]{2,1,0:T(8,128)(2,1)} %wf_in.1, bf16[2,128,128]{2,1,0:T(8,128)(2,1)} %wo_in.1), custom_call_target="tpu_custom_call" | custom-call | tf_op jit(solution)/shard_map/pallas_call | solution.py:640
  16.6 0.6 %copy.7 = bf16[4,16,128]{2,1,0:T(8,128)(2,1)} copy(bf16[4,16,128]{2,1,0:T(8,128)(2,1)S(1)} %shard_map.55) | data formatting | bytes 32768

commit v6 on v5

--- a/solution.py
+++ b/solution.py
@@ -24,6 +24,17 @@
     centred = v - jnp.mean(v, axis=-1, keepdims=True)
     r = lax.rsqrt(jnp.mean(centred * centred, axis=-1, keepdims=True) + 1e-05)
     return centred * r, r
+
+
+def scales(v):
+    mean = jnp.mean(v, axis=-1, keepdims=True)
+    centred = v - mean
+    r = lax.rsqrt(jnp.mean(centred * centred, axis=-1, keepdims=True) + 1e-05)
+    return r, r * mean
+
+
+def column_sums(w):
+    return jnp.sum(w.astype(F32), axis=0, keepdims=True)
 
 
 def norm_back(y, r, d):
@@ -190,9 +201,13 @@
     def half(ref, k0, nk):
         return ref.at[pl.ds(k0, nk), pl.ds(c0, lc)]
 
-    def projected(x, segments, weight, a_ref, b_ref, g_ref):
-        y, _ = norm(x)
-        p = dot(y, weight)
+    def projected(x, segments, weight, sums, a_ref, b_ref, g_ref):
+        r, rm = scales(x.astype(F32))
+        p = dot(x, weight)
+
+        def part(p, q):
+            return p[:, q * H : (q + 1) * H] * r - rm * sums[:, q * H : (q + 1) * H]
+
         m = jnp.concatenate([block(mask, k0, nk) for k0, nk in segments], axis=0)
         a = rounded(sigmoid(part(p, 0)) * part(p, 1) * m)
         b = rounded(sigmoid(part(p, 2)) * part(p, 3) * m)
@@ -223,6 +238,7 @@
 
     for copy in weights:
         copy.wait()
+    sums_out, sums_in, sums_mix = (column_sums(w) for w in (wf[0], wf[1], wo[0]))
     groups = [[(0, 1)], [(1, 1), (2, 2)] if rows > 2 else [(1, 1)]]
     groups += [[(d, 2)] for d in range(4, rows, 2)]
     for g, group in enumerate(groups):
@@ -237,9 +253,9 @@
             for d, count in group
         ]
         x = jnp.concatenate(
-            [x_h[pl.ds(k0, nk)].reshape(nk * lc, c).astype(F32) for k0, nk in segments], axis=0
+            [x_h[pl.ds(k0, nk)].reshape(nk * lc, c) for k0, nk in segments], axis=0
         )
-        projected(x, segments, wf[0], left, right, gate)
+        projected(x, segments, wf[0], sums_out, left, right, gate)
         for k0, nk in segments:
             partner(0, 0, half(left, k0, nk)).start()
             partner(0, 0, half(right, k0, nk)).start()
@@ -283,22 +299,34 @@
     e_out.wait_recv()
     outgoing(o0, False)
 
-    z, _ = norm(mixed[...])
+    v = mixed[...]
+    r, rm = scales(v)
+    high = v.astype(BF16)
+    low = (v - high.astype(F32)).astype(BF16)
+    update = dot(
+        jnp.concatenate([high, low], axis=1), jnp.concatenate([wo[0], wo[0]], axis=0)
+    )
     x = x_h[...].reshape(n * lc, c).astype(F32)
-    x = rounded(x + gate[...] * dot(z, wo[0]))
+    x = rounded(x + gate[...] * (update * r - rm * sums_mix))
     mid[...] = x
-    y = norm(x)[0].astype(BF16)
-    normed[...] = y
-    p = dot(y, wf[1, :, : 2 * H])
-    put_half(in_left, 0, n, rounded(sigmoid(part(p, 0)) * part(p, 1) * mask[...]))
+    r, rm = scales(x)
+
+    def scaled(p, q, at):
+        return part(p, q) * r - rm * part(sums_in, at + q)
+
+    x = x.astype(BF16)
+    normed[...] = x
+    p = dot(x, wf[1, :, : 2 * H])
+    put_half(in_left, 0, n, rounded(sigmoid(scaled(p, 0, 0)) * scaled(p, 1, 0) * mask[...]))
     e_in_left = [
         partner(1, 1 + b, in_left.at[:, pl.ds(c0 + b * TILE, TILE)]) for b in range(lc // TILE)
     ]
     for copy in e_in_left:
         copy.start()
     p = dot(normed[...], wf[1, :, 2 * H :])
-    put_half(in_right, 0, n, rounded(sigmoid(part(p, 0)) * part(p, 1) * mask[...]))
-    in_gate[...] = sigmoid(part(p, 2))
+    v = rounded(sigmoid(scaled(p, 0, 2)) * scaled(p, 1, 2) * mask[...])
+    put_half(in_right, 0, n, v)
+    in_gate[...] = sigmoid(scaled(p, 2, 2))
     e_in_right = partner(1, 3, half(in_right, 0, n))
     e_in_right.start()
 

time: 17.3 us -> 17 us (0.983)
  Pallas kernels: 16.5 us -> 16.2 us
    pallas_call x1, Pallas kernels: 16.5 us -> 16.2 us  [crop_body(): pl.pallas_call(functools.partial(crop_kernel, rows), out_shape=jax.ShapeD...]
where the time goes in v6:
time: 17 us; the launch traced here: 16.9 us
  Pallas kernels  16.2 us (95%)
  local copies, waits for them, and re-layouts  0.61 us (4%)
    pallas_call x1, Pallas kernels, crop_body(): pl.pallas_call(functools.partial(crop_kernel, rows), out_shape=jax.ShapeD...  16.2 us
    unnamed x1, local copies, waits for them, and re-layouts  0.61 us

profile of v6, /device:TPU:0, one launch (start us, length us, event | category | flops | bytes accessed | tf_op | source)
XLA Modules:
  0.0 16.9 jit_solution(8970675887792897597)
XLA Ops:
  0.0 16.2 %shard_map.55 = bf16[4,16,128]{2,1,0:T(8,128)(2,1)S(1)} custom-call(bf16[4,16,128]{2,1,0:T(8,128)(2,1)} %pair.1, bf16[4,16,128]{2,1,0:T(8,128)(2,1)} %cot.1, s32[1,32]{1,0:T(1,128)} %bitcast.1, bf16[2,128,640]{2,1,0:T(8,128)(2,1)} %wf_in.1, bf16[2,128,128]{2,1,0:T(8,128)(2,1)} %wo_in.1), custom_call_target="tpu_custom_call" | custom-call | tf_op jit(solution)/shard_map/pallas_call | solution.py:668
  16.3 0.6 %copy.7 = bf16[4,16,128]{2,1,0:T(8,128)(2,1)} copy(bf16[4,16,128]{2,1,0:T(8,128)(2,1)S(1)} %shard_map.55) | data formatting | bytes 32768

commit v7 on v6

--- a/solution.py
+++ b/solution.py
@@ -77,11 +77,11 @@
 
 def crop_kernel(
     rows, pair, cot, mask_in, wf_in, wo_in, out,
-    x_h, ct_h, wf, wo, chain,
+    x_h, ct_h, x_far, wf, wo, chain,
     left, right, in_left, in_right, sig, left_t, right_t, flip_r, flip_s,
     mask, mixed, gate, mid, in_mixed, in_gate, ct32, normed, along,
     saved, d_left, d_right, sig_row, sig_col,
-    local_sem, x_send, x_recv, ct_send, ct_recv, psend, precv, ready,
+    local_sem, x_send, x_recv, ct_send, ct_recv, psend, precv, ready, far_send, far_recv,
 ):
     n, c = left.shape[0], left.shape[2]
     lr, lc = out.shape[0], out.shape[1]
@@ -97,12 +97,22 @@
             total = total + (1 - bit if d >> b & 1 else bit) * (1 << b)
         return total
 
+    far = rows - 2 if rows > 4 else rows
+    wide_row = jnp.logical_and(me >= far, my_col == 0)
+    near_row = jnp.logical_and(me == 0, rows > 4)
     barrier = pltpu.get_barrier_semaphore()
     pl.semaphore_signal(barrier, inc=1, device_id={"col": other}, device_id_type=MESH)
     for row in range(1, rows):
-        @pl.when(me < row)
+        @pl.when(jnp.logical_and(me < row, me != row - 1) if row == far else me < row)
         def _():
             pl.semaphore_signal(barrier, inc=1, device_id={"row": row}, device_id_type=MESH)
+
+    for row in range(far, rows):
+        @pl.when(jnp.logical_and(me == 0, my_col == 1))
+        def _():
+            pl.semaphore_signal(
+                barrier, inc=1, device_id={"row": row, "col": 0}, device_id_type=MESH
+            )
 
     r0 = pl.multiple_of(me * lr, lr)
     c0 = pl.multiple_of(my_col * lc, lc)
@@ -134,20 +144,35 @@
             device_id_type=MESH,
         )
 
-    def lower(step):
-        for row in range(rows - 1):
-            @pl.when(row < me)
+    def lower(step, start=0):
+        for row in range(start, rows - 1):
+            @pl.when(jnp.logical_and(row < me, me != far) if row == far - 1 else row < me)
             def _():
                 step(row)
 
     def higher(step):
         for row in range(1, rows):
-            @pl.when(row > me)
+            @pl.when(jnp.logical_or(row > me, me == far) if row == far - 1 else row > me)
             def _():
                 step(row)
 
+    def far_copy():
+        at = pl.ds(pl.multiple_of((me - far) * lr, lr), lr)
+        return pltpu.make_async_remote_copy(
+            src_ref=pair,
+            dst_ref=x_far.at[at],
+            send_sem=far_send.at[0],
+            recv_sem=far_recv.at[me - far],
+            device_id={"row": 0, "col": 1},
+            device_id_type=MESH,
+        )
+
     def answer(row):
-        if row < 2:
+        if row == 0:
+            @pl.when(jnp.logical_not(wide_row))
+            def _():
+                direct(0, row, me).start()
+        elif row < 2:
             direct(0, row, me).start()
         pl.semaphore_signal(ready.at[me], inc=1, device_id={"row": row}, device_id_type=MESH)
 
@@ -155,9 +180,17 @@
         if row >= 2:
             direct(0, row, me).start()
 
+    def tell(row, about):
+        pl.semaphore_signal(ready.at[about], inc=1, device_id={"row": row}, device_id_type=MESH)
+
     def follow(row):
         pl.semaphore_wait(ready.at[row], 1)
         direct(0, row, me).start()
+        if row == far:
+            @pl.when(me == far - 2)
+            def _():
+                tell(far, far - 1)
+                tell(far - 1, far)
 
     def drain(row):
         direct(0, row, me).wait_send()
@@ -175,7 +208,14 @@
             device_id_type=MESH,
         )
 
-    pl.semaphore_wait(barrier, me + 1)
+    greeted = me + 1 - jnp.where(me == far, 1, 0)
+    pl.semaphore_wait(barrier, greeted + jnp.where(wide_row, 1, 0))
+
+    @pl.when(wide_row)
+    def _():
+        direct(0, 0, me).start()
+        far_copy().start()
+
     lower(answer)
 
     chain_copy.wait()
@@ -256,17 +296,28 @@
             [x_h[pl.ds(k0, nk)].reshape(nk * lc, c) for k0, nk in segments], axis=0
         )
         projected(x, segments, wf[0], sums_out, left, right, gate)
-        for k0, nk in segments:
-            partner(0, 0, half(left, k0, nk)).start()
-            partner(0, 0, half(right, k0, nk)).start()
+        def exchange():
+            for k0, nk in segments:
+                partner(0, 0, half(left, k0, nk)).start()
+                partner(0, 0, half(right, k0, nk)).start()
+
+        if g == len(groups) - 1 and rows > 4:
+            pl.when(jnp.logical_not(jnp.logical_and(near_row, my_col == 0)))(exchange)
+        else:
+            exchange()
         if g == 0:
             higher(follow)
+
+            @pl.when(me > 0)
+            def _():
+                second(0)
+
             lower(drain)
             pl.semaphore_signal(
                 ready.at[rows], inc=1, device_id={"col": other}, device_id_type=MESH
             )
             pl.semaphore_wait(ready.at[rows], 1)
-            lower(second)
+            lower(second, 1)
         if g == len(groups) - 1:
             higher(second)
 
@@ -295,8 +346,43 @@
         loop(n // group, step)
 
     outgoing(c0, True)
-    e_out = partner(0, 0, left)
-    e_out.wait_recv()
+
+    @pl.when(jnp.logical_and(near_row, my_col == 1))
+    def _():
+        for q in range(2):
+            pltpu.make_async_remote_copy(
+                src_ref=pair,
+                dst_ref=x_far.at[pl.ds(q * lr, lr)],
+                send_sem=far_send.at[0],
+                recv_sem=far_recv.at[q],
+                device_id={"row": 0, "col": 0},
+                device_id_type=MESH,
+            ).wait_recv()
+        x = x_far[...].reshape(2 * lr * lc, c)
+        r, rm = scales(x.astype(F32))
+        p = dot(x, wf[0, :, : 4 * H])
+
+        def scaled(q):
+            return part(p, q) * r - rm * part(sums_out, q)
+
+        k0 = far * lr
+        over = along[pl.ds(o0, lc), :]
+        m = jnp.concatenate([over * along[k0 + i : k0 + i + 1] for i in range(2 * lr)], axis=0)
+        a = rounded(sigmoid(scaled(0)) * scaled(1) * m)
+        b = rounded(sigmoid(scaled(2)) * scaled(3) * m)
+        left[k0:, pl.ds(o0, lc), :] = a.reshape(2 * lr, lc, c)
+        right[k0:, pl.ds(o0, lc), :] = b.reshape(2 * lr, lc, c)
+
+    def pair_bytes(column, step):
+        @pl.when(jnp.logical_and(near_row, my_col == column))
+        def _():
+            step(partner(0, 0, left.at[pl.ds(0, far * lr)]))
+
+        @pl.when(jnp.logical_not(jnp.logical_and(near_row, my_col == column)))
+        def _():
+            step(partner(0, 0, left))
+
+    pair_bytes(1, lambda copy: copy.wait_recv())
     outgoing(o0, False)
 
     v = mixed[...]
@@ -532,7 +618,13 @@
 
     higher(drain)
     e_ct.wait_send()
-    for copy in (e_out, partner(1, 3, in_left), e_sig, e_row):
+    pair_bytes(0, lambda copy: copy.wait_send())
+
+    @pl.when(wide_row)
+    def _():
+        far_copy().wait_send()
+
+    for copy in (partner(1, 3, in_left), e_sig, e_row):
         copy.wait_send()
 
     @pl.when(owner)
@@ -673,6 +765,7 @@
         scratch_shapes=[
             pltpu.VMEM((n, lc, c), BF16),
             pltpu.VMEM((n, lc, c), BF16),
+            pltpu.VMEM((2 * lr, lc, c), BF16),
             pltpu.VMEM(front_weight.shape, BF16),
             pltpu.VMEM(out_weight.shape, BF16),
             pltpu.VMEM((1, n), jnp.int32),
@@ -690,7 +783,7 @@
             pltpu.VMEM((lr, n, c), F32),
         ]
         + [dma((5,)), dma((rows,)), dma((rows,)), dma((1,)), dma((1,)), dma((5,)), dma((7,))]
-        + [pltpu.SemaphoreType.REGULAR((rows + 1,))],
+        + [pltpu.SemaphoreType.REGULAR((rows + 1,)), dma((1,)), dma((2,))],
         compiler_params=pltpu.CompilerParams(
             collective_id=0, has_side_effects=True, vmem_limit_bytes=VMEM_BUDGET
         ),

time: 17 us -> 16.5 us (0.971)
  Pallas kernels: 16.2 us -> 15.6 us
    pallas_call x1, Pallas kernels: 16.2 us -> 15.6 us  [crop_body(): pl.pallas_call(functools.partial(crop_kernel, rows), out_shape=jax.ShapeD...]
where the time goes in v7:
time: 16.5 us; the launch traced here: 16.2 us
  Pallas kernels  15.6 us (95%)
  local copies, waits for them, and re-layouts  0.61 us (4%)
    pallas_call x1, Pallas kernels, crop_body(): pl.pallas_call(functools.partial(crop_kernel, rows), out_shape=jax.ShapeD...  15.6 us
    unnamed x1, local copies, waits for them, and re-layouts  0.61 us

profile of v7, /device:TPU:0, one launch (start us, length us, event | category | flops | bytes accessed | tf_op | source)
XLA Modules:
  0.0 16.2 jit_solution(5114130122819526218)
XLA Ops:
  0.0 15.6 %shard_map.55 = bf16[4,16,128]{2,1,0:T(8,128)(2,1)S(1)} custom-call(bf16[4,16,128]{2,1,0:T(8,128)(2,1)} %pair.1, bf16[4,16,128]{2,1,0:T(8,128)(2,1)} %cot.1, s32[1,32]{1,0:T(1,128)} %bitcast.1, bf16[2,128,640]{2,1,0:T(8,128)(2,1)} %wf_in.1, bf16[2,128,128]{2,1,0:T(8,128)(2,1)} %wo_in.1), custom_call_target="tpu_custom_call" | custom-call | tf_op jit(solution)/shard_map/pallas_call | solution.py:760
  15.6 0.6 %copy.7 = bf16[4,16,128]{2,1,0:T(8,128)(2,1)} copy(bf16[4,16,128]{2,1,0:T(8,128)(2,1)S(1)} %shard_map.55) | data formatting | bytes 32768
